TPU v7x, 32 devices: a whole 2x2x4 slice. The times are simulated.
32 devices in a mesh: dp: 8 (over y, x, core), mp: 4 (over z).
Axes of the slice: x: 2, y: 2, z: 4, core: 2. Of those that a mesh axis runs over, the one named last changes fastest.
Arguments:
- tokens: bfloat16 [16384, 768], P('dp'), may hold values from -6 to 6
- cotangent: bfloat16 [16384, 768], P('dp'), may hold values from -6 to 6
- random_blocks: int32 [16, 12, 14, 3], P('dp', 'mp'), may hold values from 1 to 14
- query_weight: bfloat16 [768, 768], P(None, 'mp'), may hold values from -0.21875 to 0.21875
- query_bias: bfloat16 [768], P('mp'), may hold values from -3 to 3
- key_weight: bfloat16 [768, 768], P(None, 'mp'), may hold values from -0.21875 to 0.21875
- value_weight: bfloat16 [768, 768], P(None, 'mp'), may hold values from -0.21875 to 0.21875
- value_bias: bfloat16 [768], P('mp'), may hold values from -0.59765625 to 0.59765625
- out_weight: bfloat16 [768, 768], P('mp'), may hold values from -1.75 to 1.75
- out_bias: bfloat16 [768], replicated, may hold values from -2 to 2
- attn_gain: bfloat16 [768], replicated, may hold values from 0.099609375 to 1.8984375
- attn_shift: bfloat16 [768], replicated, may hold values from -2 to 2
- up_weight: bfloat16 [768, 3072], P(None, 'mp'), may hold values from -0.21875 to 0.21875
- up_bias: bfloat16 [3072], P('mp'), may hold values from -3 to 3
- down_weight: bfloat16 [3072, 768], P('mp'), may hold values from -0.21875 to 0.21875
- down_bias: bfloat16 [768], replicated, may hold values from -2 to 2
- mlp_gain: bfloat16 [768], replicated, may hold values from 0.099609375 to 1.8984375
- mlp_shift: bfloat16 [768], replicated, may hold values from -2 to 2
Outputs:
- layer_out: float32 [16384, 768], P('dp')
- tokens_grad: float32 [16384, 768], P('dp')
- grad_query_weight: float32 [768, 768], P(None, 'mp')
- grad_query_bias: float32 [768], P('mp')
- grad_key_weight: float32 [768, 768], P(None, 'mp')
- grad_value_weight: float32 [768, 768], P(None, 'mp')
- grad_value_bias: float32 [768], P('mp')
- grad_out_weight: float32 [768, 768], P('mp')
- grad_out_bias: float32 [768], replicated
- grad_attn_gain: float32 [768], replicated
- grad_attn_shift: float32 [768], replicated
- grad_up_weight: float32 [768, 3072], P(None, 'mp')
- grad_up_bias: float32 [3072], P('mp')
- grad_down_weight: float32 [3072, 768], P('mp')
- grad_down_bias: float32 [768], replicated
- grad_mlp_gain: float32 [768], replicated
- grad_mlp_shift: float32 [768], replicated
All inputs are finite; a program needn't handle non-finite values.
Results may differ from a plain program's by a relative error of at most 0.014.
The roundings to bfloat16 on the way count: a program that leaves them out, or rounds other values in their place, can miss the bound.
Values sent between devices are 32-bit elements; how exact they have to be, the bound alone decides.
A program may use at most 256 MiB of HBM per device.

v0:
```python
import jax
import jax.numpy as jnp
from jax import lax
from jax.sharding import PartitionSpec as P

HEAD_DIM = 64
BLOCK = 64
LEN = 1024
EPSILON = 1e-05
SCALING = 0.125
MIDDLE_FORMS = ("shmqd,shmkd->shmqk", "shmqk,shmkd->shmqd", "shmqk,shmqd->shmkd")
GLOBAL_FORMS = ("shgqd,shkd->shgqk", "shgqk,shkd->shgqd", "shgqk,shgqd->shkd")


def contract_rows(left, right):
    return lax.dot_general(
        left, right, (((0,), (0,)), ((), ())), preferred_element_type=jnp.float32
    )


def apply_rows(left, weight):
    return lax.dot_general(
        left, weight, (((1,), (1,)), ((), ())), preferred_element_type=jnp.float32
    )


def norm_stats(summed):
    row_mean = jnp.mean(summed, -1, keepdims=True)
    centered = summed - row_mean
    scaling = lax.rsqrt(jnp.mean(centered * centered, -1, keepdims=True) + EPSILON)
    return (centered * scaling, scaling)


def norm_back(grad_result, normed, scaling, scale_gain):
    grad_normed = grad_result * scale_gain
    inner_mean = jnp.mean(grad_normed, -1, keepdims=True)
    cross_mean = jnp.mean(grad_normed * normed, -1, keepdims=True)
    return scaling * (grad_normed - inner_mean - normed * cross_mean)


def finish_norm(partial_sum, residual, bias_value, which):
    if which == "attn":
        summed = lax.psum(partial_sum, "mp")
    else:
        summed = lax.psum(partial_sum, "mp")
    result = norm_stats(residual + (summed + bias_value))
    return result


def to_heads(flat, seq_count):
    head_count = flat.shape[1] // HEAD_DIM
    return flat.reshape(seq_count, LEN // BLOCK, BLOCK, head_count, HEAD_DIM).transpose(
        0, 3, 1, 2, 4
    )


def from_heads(split):
    seq_count, head_count, block_count, block_rows, head_dim = split.shape
    return split.transpose(0, 2, 3, 1, 4).reshape(
        seq_count * block_count * block_rows, head_count * head_dim
    )


def key_blocks(random_blocks):
    block_count = LEN // BLOCK
    middle = jnp.arange(1, block_count - 1, dtype=jnp.int32)
    fixed = jnp.stack(
        [
            middle - 1,
            middle,
            middle + 1,
            jnp.zeros_like(middle),
            jnp.full_like(middle, block_count - 1),
        ],
        1,
    )
    fixed = jnp.broadcast_to(fixed, random_blocks.shape[:2] + fixed.shape)
    return jnp.concatenate([fixed, random_blocks], 3)


def pick_blocks(blocks, chosen):
    picked = jax.vmap(jax.vmap(lambda source, listed: source[listed]))(blocks, chosen)
    seq_count, head_count, middle_count, listed_count, block_rows, head_dim = picked.shape
    return picked.reshape(seq_count, head_count, middle_count, listed_count * block_rows, head_dim)


def soft_forward(queries, key_rows, value_rows, forms):
    scores = jnp.einsum(forms[0], queries, key_rows, preferred_element_type=jnp.float32) * SCALING
    highest = jnp.max(scores, -1, keepdims=True)
    summed = jnp.sum(jnp.exp(scores - highest), -1, keepdims=True)
    logsum = highest + jnp.log(summed)
    soft_low = jnp.exp(scores - logsum).astype(jnp.bfloat16)
    return (jnp.einsum(forms[1], soft_low, value_rows, preferred_element_type=jnp.float32), logsum)


def soft_back(queries, key_rows, value_rows, logsum, grad_out, forms):
    scores = jnp.einsum(forms[0], queries, key_rows, preferred_element_type=jnp.float32) * SCALING
    soft = jnp.exp(scores - logsum)
    grad_soft = jnp.einsum(forms[0], grad_out, value_rows, preferred_element_type=jnp.float32)
    row_inner = jnp.sum(soft * grad_soft, -1, keepdims=True)
    grad_scores = (soft * (grad_soft - row_inner)).astype(jnp.bfloat16)
    grad_values = jnp.einsum(
        forms[2], soft.astype(jnp.bfloat16), grad_out, preferred_element_type=jnp.float32
    )
    grad_queries = (
        jnp.einsum(forms[1], grad_scores, key_rows, preferred_element_type=jnp.float32) * SCALING
    )
    grad_keys = (
        jnp.einsum(forms[2], grad_scores, queries, preferred_element_type=jnp.float32) * SCALING
    )
    return (grad_queries, grad_keys, grad_values)


def global_rows(split):
    block_count = split.shape[2]
    return jnp.stack([split[:, :, 0], split[:, :, block_count - 1]], 2)


def flat_keys(split):
    seq_count, head_count, block_count, block_rows, head_dim = split.shape
    return split.reshape(seq_count, head_count, block_count * block_rows, head_dim)


def attend_all(queries, key_rows, value_rows, chosen):
    block_count = queries.shape[2]
    out_middle, log_middle = soft_forward(
        queries[:, :, 1 : block_count - 1],
        pick_blocks(key_rows, chosen),
        pick_blocks(value_rows, chosen),
        MIDDLE_FORMS,
    )
    out_global, log_global = soft_forward(
        global_rows(queries), flat_keys(key_rows), flat_keys(value_rows), GLOBAL_FORMS
    )
    attended = jnp.concatenate([out_global[:, :, 0:1], out_middle, out_global[:, :, 1:2]], 2)
    return (attended, (log_middle, log_global))


def attend_back(queries, key_rows, value_rows, chosen, logsums, grad_out):
    block_count = queries.shape[2]
    grad_middle_q, grad_listed_k, grad_listed_v = soft_back(
        queries[:, :, 1 : block_count - 1],
        pick_blocks(key_rows, chosen),
        pick_blocks(value_rows, chosen),
        logsums[0],
        grad_out[:, :, 1 : block_count - 1],
        MIDDLE_FORMS,
    )
    grad_global_q, grad_all_k, grad_all_v = soft_back(
        global_rows(queries),
        flat_keys(key_rows),
        flat_keys(value_rows),
        logsums[1],
        global_rows(grad_out),
        GLOBAL_FORMS,
    )
    onehot = (chosen[..., None] == jnp.arange(block_count, dtype=jnp.int32)).astype(jnp.float32)
    split_shape = chosen.shape + (queries.shape[3], queries.shape[4])
    grad_keys = jnp.einsum(
        "shmcn,shmckd->shnkd",
        onehot,
        grad_listed_k.reshape(split_shape),
        precision=lax.Precision.HIGHEST,
    ) + grad_all_k.reshape(queries.shape)
    grad_values = jnp.einsum(
        "shmcn,shmckd->shnkd",
        onehot,
        grad_listed_v.reshape(split_shape),
        precision=lax.Precision.HIGHEST,
    ) + grad_all_v.reshape(queries.shape)
    grad_queries = jnp.concatenate(
        [grad_global_q[:, :, 0:1], grad_middle_q, grad_global_q[:, :, 1:2]], 2
    )
    return (grad_queries, grad_keys, grad_values)


def column_sum(values_low):
    return jnp.sum(values_low.astype(jnp.float32), 0)


def on_device(
    tokens,
    cotangent,
    random_blocks,
    query_weight,
    query_bias,
    key_weight,
    value_weight,
    value_bias,
    out_weight,
    out_bias,
    attn_gain,
    attn_shift,
    up_weight,
    up_bias,
    down_weight,
    down_bias,
    mlp_gain,
    mlp_shift,
):
    seq_count = tokens.shape[0] // LEN
    residual = tokens.astype(jnp.float32)
    queries = (
        jnp.dot(tokens, query_weight, preferred_element_type=jnp.float32)
        + query_bias.astype(jnp.float32)
    ).astype(jnp.bfloat16)
    key_rows = jnp.dot(tokens, key_weight, preferred_element_type=jnp.float32).astype(jnp.bfloat16)
    value_rows = (
        jnp.dot(tokens, value_weight, preferred_element_type=jnp.float32)
        + value_bias.astype(jnp.float32)
    ).astype(jnp.bfloat16)
    query_heads = to_heads(queries, seq_count)
    key_heads = to_heads(key_rows, seq_count)
    value_heads = to_heads(value_rows, seq_count)
    chosen = key_blocks(random_blocks)
    attended, logsums = attend_all(query_heads, key_heads, value_heads, chosen)
    attended_low = from_heads(attended).astype(jnp.bfloat16)
    attn_partial = jnp.dot(attended_low, out_weight, preferred_element_type=jnp.float32)
    normed_attn, scale_attn = finish_norm(
        attn_partial, residual, out_bias.astype(jnp.float32), "attn"
    )
    gain_one = attn_gain.astype(jnp.float32)
    hidden = normed_attn * gain_one + attn_shift.astype(jnp.float32)
    hidden_low = hidden.astype(jnp.bfloat16)
    up_value = jnp.dot(hidden_low, up_weight, preferred_element_type=jnp.float32) + up_bias.astype(
        jnp.float32
    )
    active, gelu_pull = jax.vjp(lambda entry: jax.nn.gelu(entry, approximate=True), up_value)
    active_low = active.astype(jnp.bfloat16)
    mlp_partial = jnp.dot(active_low, down_weight, preferred_element_type=jnp.float32)
    normed_mlp, scale_mlp = finish_norm(mlp_partial, hidden, down_bias.astype(jnp.float32), "mlp")
    gain_two = mlp_gain.astype(jnp.float32)
    layer_out = normed_mlp * gain_two + mlp_shift.astype(jnp.float32)
    grad_result = cotangent.astype(jnp.float32)
    grad_mlp_gain = jnp.sum(grad_result * normed_mlp, 0)
    grad_mlp_shift = jnp.sum(grad_result, 0)
    grad_mlp_in = norm_back(grad_result, normed_mlp, scale_mlp, gain_two)
    grad_mlp_low = grad_mlp_in.astype(jnp.bfloat16)
    grad_down_bias = column_sum(grad_mlp_low)
    grad_down_weight = contract_rows(active_low, grad_mlp_low)
    grad_active = apply_rows(grad_mlp_low, down_weight)
    grad_up_value = gelu_pull(grad_active)[0].astype(jnp.bfloat16)
    grad_up_bias = column_sum(grad_up_value)
    grad_up_weight = contract_rows(hidden_low, grad_up_value)
    mlp_terms = (
        grad_up_weight,
        grad_up_bias,
        grad_down_weight,
        grad_down_bias,
        grad_mlp_gain,
        grad_mlp_shift,
    )
    back_hidden = lax.psum(apply_rows(grad_up_value, up_weight), "mp")
    grad_hidden = grad_mlp_in + back_hidden
    grad_attn_gain = jnp.sum(grad_hidden * normed_attn, 0)
    grad_attn_shift = jnp.sum(grad_hidden, 0)
    grad_attn_in = norm_back(grad_hidden, normed_attn, scale_attn, gain_one)
    grad_attn_low = grad_attn_in.astype(jnp.bfloat16)
    grad_out_bias = column_sum(grad_attn_low)
    grad_out_weight = contract_rows(attended_low, grad_attn_low)
    grad_attended = apply_rows(grad_attn_low, out_weight).astype(jnp.bfloat16)
    grad_q_heads, grad_k_heads, grad_v_heads = attend_back(
        query_heads, key_heads, value_heads, chosen, logsums, to_heads(grad_attended, seq_count)
    )
    grad_queries = from_heads(grad_q_heads).astype(jnp.bfloat16)
    grad_keys = from_heads(grad_k_heads).astype(jnp.bfloat16)
    grad_values = from_heads(grad_v_heads).astype(jnp.bfloat16)
    grad_query_weight = contract_rows(tokens, grad_queries)
    grad_query_bias = column_sum(grad_queries)
    grad_key_weight = contract_rows(tokens, grad_keys)
    grad_value_weight = contract_rows(tokens, grad_values)
    grad_value_bias = column_sum(grad_values)
    back_tokens = lax.psum(
        apply_rows(grad_queries, query_weight)
        + apply_rows(grad_keys, key_weight)
        + apply_rows(grad_values, value_weight),
        "mp",
    )
    tokens_grad = grad_attn_in + back_tokens
    attn_terms = (
        grad_query_weight,
        grad_query_bias,
        grad_key_weight,
        grad_value_weight,
        grad_value_bias,
        grad_out_weight,
        grad_out_bias,
        grad_attn_gain,
        grad_attn_shift,
    )
    summed_all = lax.psum(attn_terms + mlp_terms, "dp")
    attn_terms = summed_all[:9]
    mlp_terms = summed_all[9:]
    return (
        layer_out,
        tokens_grad,
        attn_terms[0],
        attn_terms[1],
        attn_terms[2],
        attn_terms[3],
        attn_terms[4],
        attn_terms[5],
        attn_terms[6],
        attn_terms[7],
        attn_terms[8],
        mlp_terms[0],
        mlp_terms[1],
        mlp_terms[2],
        mlp_terms[3],
        mlp_terms[4],
        mlp_terms[5],
    )


def solution(mesh):
    return jax.shard_map(
        on_device,
        mesh=mesh,
        in_specs=(
            P("dp", None),
            P("dp", None),
            P("dp", "mp", None, None),
            P(None, "mp"),
            P("mp"),
            P(None, "mp"),
            P(None, "mp"),
            P("mp"),
            P("mp", None),
            P(),
            P(),
            P(),
            P(None, "mp"),
            P("mp"),
            P("mp", None),
            P(),
            P(),
            P(),
        ),
        out_specs=(
            P("dp", None),
            P("dp", None),
            P(None, "mp"),
            P("mp"),
            P(None, "mp"),
            P(None, "mp"),
            P("mp"),
            P("mp", None),
            P(),
            P(),
            P(),
            P(None, "mp"),
            P("mp"),
            P("mp", None),
            P(),
            P(),
            P(),
        ),
        check_vma=False,
    )
```

profile of v0, /device:TPU:0, one launch (start us, length us, event | category | flops | bytes accessed | tf_op | source)
XLA Modules:
  0.0 1423.7 jit_solution(11912262535709834846)
XLA Ops:
  38.2 14.0 gather_fusion
  52.2 15.7 %gather_fusion.1 = bf16[672,64,64]{2,1,0:T(8,128)(2,1)} fusion(bf16[2,3,16,64,64]{4,3,2,1,0:T(8,128)(2,1)} %bitcast.159, s32[672]{0:T(1024)S(1)} %reshape.248), kind=kCustom, calls=%fused_computation.1 | custom fusion | bytes 11018112 | tf_op jit(solution)/shard_map/vmap(vmap())/gather | solution.py:82
  67.9 12.1 multiply_reduce_fusion.1
  80.1 5.9 exponential_reduce_fusion
  86.0 9.5 convolution_convert_fusion.2
  104.8 225.6 %all-reduce.8.cloned.1.call-done = f32[2048,768]{1,0:T(8,128)} async-done(((f32[2048,768]{1,0:T(8,128)}), f32[2048,768]{1,0:T(8,128)}) %all-reduce.8.cloned.1.call-update) | async-done | bytes 6291472 | tf_op jit(solution)/shard_map/psum | solution.py:43
  330.4 4.6 fusion.64
  344.7 5.9 fusion.61
  351.2 221.2 %all-reduce.10.cloned.1.call-done = f32[2048,768]{1,0:T(8,128)} async-done(((f32[2048,768]{1,0:T(8,128)}), f32[2048,768]{1,0:T(8,128)}) %all-reduce.10.cloned.1.call-update) | async-done | bytes 6291472 | tf_op jit(solution)/shard_map/psum | solution.py:45
  572.5 5.7 fusion.63
  583.7 4.9 convert_reduce_fusion.1
  588.7 7.1 convert_reduce_fusion.2
  602.8 221.1 %all-reduce.12.cloned.1.call-done = f32[2048,768]{1,0:T(8,128)} async-done(((f32[2048,768]{1,0:T(8,128)}), f32[2048,768]{1,0:T(8,128)}) %all-reduce.12.cloned.1.call-update) | async-done | bytes 6291472 | tf_op jit(solution)/shard_map/psum | solution.py:253
  823.9 9.1 multiply_reduce_fusion.2
  833.0 5.2 convert_reduce_fusion.3
  846.0 12.5 multiply_reduce_fusion
  858.4 10.9 fusion.22
  877.9 7.1 multiply_convert_fusion
  887.2 7.2 broadcast_multiply_fusion
  921.5 16.6 %reshape.244 = f32[2,3,14,8,64,64]{4,3,5,2,1,0:T(8,128)} reshape(f32[2,3,14,512,64]{3,4,2,1,0:T(8,128)} %broadcast_multiply_fusion) | data formatting | bytes 22020096 | tf_op jit(solution)/shard_map/reshape | solution.py:162
  938.1 26.6 %copy.68 = f32[2,3,14,8,64,64]{5,2,3,4,1,0:T(8,128)} copy(f32[2,3,14,8,64,64]{4,3,5,2,1,0:T(8,128)} %reshape.244) | data formatting | bytes 22020096 | tf_op jit(solution)/shard_map/reshape | solution.py:162
  964.8 15.6 %fusion.21 = bf16[2,16,64,3,64]{4,1,2,3,0:T(8,128)(2,1)} fusion(f32[2,3,16,64,64]{4,2,3,1,0:T(8,128)} %copy.70, f32[2,3,14,8,64,64]{5,2,3,4,1,0:T(8,128)} %copy.68, s32[2,3,14,8]{2,3,1,0:T(8,128)S(1)} %pad_add_fusion), kind=kOutput, calls=%fused_computation.69 | convolution fusion | flops 529279488 | bytes 13372032 | tf_op jit(solution)/shard_map/shmcn,shmckd->shnkd/dot_general | solution.py:159
  991.0 16.6 %reshape.246 = f32[2,3,14,8,64,64]{4,3,5,2,1,0:T(8,128)} reshape(f32[2,3,14,512,64]{3,4,2,1,0:T(8,128)} %fusion.22) | data formatting | bytes 22020096 | tf_op jit(solution)/shard_map/reshape | solution.py:168
  1007.6 26.4 %copy.73 = f32[2,3,14,8,64,64]{5,2,3,4,1,0:T(8,128)} copy(f32[2,3,14,8,64,64]{4,3,5,2,1,0:T(8,128)} %reshape.246) | data formatting | bytes 22020096 | tf_op jit(solution)/shard_map/reshape | solution.py:168
  1034.1 17.9 %convert_reduce_fusion.4 = (f32[3,64]{1,0:T(4,128)S(1)}, bf16[2,3,16,64,64]{4,2,3,1,0:T(8,128)(2,1)}) fusion(f32[2,3,16,64,64]{4,2,3,1,0:T(8,128)} %copy.75, f32[2,3,14,8,64,64]{5,2,3,4,1,0:T(8,128)} %copy.73, s32[2,3,14,8]{2,3,1,0:T(8,128)S(1)} %pad_add_fusion), kind=kOutput, calls=%fused_computation.51 | convolution fusion | flops 530065728 | bytes 13372800 | tf_op jit(solution)/shard_map/shmcn,shmckd->shnkd/dot_general | solution.py:165
  1058.9 8.6 add_add_fusion
  1067.8 6.9 fusion.74
  1074.7 9.7 fusion.50
  1091.7 26.0 %all-reduce = (f32[192]{0:T(256)}, f32[192]{0:T(256)}, f32[768]{0:T(1024)}, f32[768]{0:T(1024)}, f32[768]{0:T(1024)}, /*index=5*/f32[768]{0:T(1024)}, f32[768]{0:T(1024)}, f32[768]{0:T(1024)}, f32[768]{0:T(1024)}) all-reduce(f32[192]{0:T(256)S(1)} %reduce_sum.206, f32[192]{0:T(256)S(1)} %reduce_sum.208, ...), channel_id=1, replica_groups=mesh['dp'=8,'mp'=4] {'dp'}, use_global_device_ids=true, to_apply=%region_20.0 | all-reduce | flops 5760 | bytes 46080 | tf_op jit(solution)/shard_map/psum | solution.py:291
  1117.8 171.7 %all-reduce.14.cloned.1.call-done = f32[2048,768]{1,0:T(8,128)} async-done(((f32[2048,768]{1,0:T(8,128)}), f32[2048,768]{1,0:T(8,128)}) %all-reduce.14.cloned.1.call-update) | async-done | bytes 6291472 | tf_op jit(solution)/shard_map/psum | solution.py:273
  1289.4 8.1 add.232
  1297.5 108.7 %all-reduce.16.cloned.1.call-done = (f32[768,192]{0,1:T(8,128)}, f32[768,192]{0,1:T(8,128)}, f32[768,192]{0,1:T(8,128)}, f32[192,768]{1,0:T(8,128)}, f32[768,768]{1,0:T(8,128)}, /*index=5*/f32[768,768]{1,0:T(8,128)}) async-done(((f32[768,192]{0,1:T(8,128)}, f32[768,192]{0,1:T(8,128)}, f32[768,192]{0,1:T(8,128)}, f32[192,768]{1,0:T(8,128)}, f32[768,768]{1,0:T(8,128)}, /*index=5*/f32[768,768]{1,0:T(8,128)}), ...) | async-done | bytes 7077904 | tf_op jit(solution)/shard_map/psum | solution.py:291
  (239 shorter events, 144.0 us)
Async XLA Ops:
  7.2 337.5 %copy-start = (bf16[768,768]{1,0:T(8,128)(2,1)S(1)}, bf16[768,768]{1,0:T(8,128)(2,1)}, u32[]{:S(2)}) copy-start(bf16[768,768]{1,0:T(8,128)(2,1)} %param.32) | copy-start | bytes 3538948
  7.2 323.2 %all-reduce.8.cloned.1.call-start = ((), (), s32[]{:S(2)}) async-start(), calls=%async_computation | async-start | bytes 12582912 | tf_op jit(solution)/shard_map/psum | solution.py:43
  17.7 17.1 %copy-start.26 = (bf16[2,3,1,64,64]{4,3,2,1,0:T(8,128)(2,1)}, bf16[2,3,1,64,64]{4,3,2,1,0:T(8,128)(2,1)S(1)}, u32[]{:S(2)}) copy-start(bf16[2,3,1,64,64]{4,3,2,1,0:T(8,128)(2,1)S(1)} %get-tuple-element.52) | copy-start | bytes 147460
  17.8 17.1 %copy-start.28 = (bf16[2,3,1,64,64]{4,3,2,1,0:T(8,128)(2,1)}, bf16[2,3,1,64,64]{4,3,2,1,0:T(8,128)(2,1)S(1)}, u32[]{:S(2)}) copy-start(bf16[2,3,1,64,64]{4,3,2,1,0:T(8,128)(2,1)S(1)} %get-tuple-element.53) | copy-start | bytes 147460
  17.8 9.0 copy-start.31
  52.2 15.7 %copy-start.21 = (bf16[2,16,64,3,64]{4,2,1,3,0:T(8,128)(2,1)S(1)}, bf16[2,16,64,3,64]{4,2,1,3,0:T(8,128)(2,1)}, u32[]{:S(2)}) copy-start(bf16[2,16,64,3,64]{4,2,1,3,0:T(8,128)(2,1)} %copy.48) | copy-start | bytes 2359300
  95.5 5.3 copy-start.25
  104.7 467.8 %all-reduce.10.cloned.1.call-start = ((), (), s32[]{:S(2)}) async-start(), calls=%async_computation.1 | async-start | bytes 12582912 | tf_op jit(solution)/shard_map/psum | solution.py:45
  104.8 483.9 %copy-start.44 = (f32[768]{0:T(1024)}, f32[768]{0:T(1024)S(1)}, u32[]{:S(2)}) copy-start(f32[768]{0:T(1024)S(1)} %convert_element_type.146) | copy-start | bytes 9220
  350.5 473.4 %all-reduce.12.cloned.1.call-start = ((), (), s32[]{:S(2)}) async-start(), calls=%async_computation.2 | async-start | bytes 12582912 | tf_op jit(solution)/shard_map/psum | solution.py:253
  580.0 8.6 slice-start.8
  588.6 7.1 copy-start.11
  602.0 687.4 %all-reduce.14.cloned.1.call-start = ((), (), s32[]{:S(2)}) async-start(), calls=%async_computation.3 | async-start | bytes 12582912 | tf_op jit(solution)/shard_map/psum | solution.py:273
  858.4 12.0 copy-start.8
  858.4 12.0 copy-start.35
  874.3 10.8 slice-start.5
  877.9 7.1 slice-start.6
  877.9 7.1 slice-start.7
  901.8 16.0 %copy-start.15 = (bf16[2048,192]{0,1:T(8,128)(2,1)}, bf16[2048,192]{0,1:T(8,128)(2,1)S(1)}, u32[]{:S(2)}) copy-start(bf16[2048,192]{0,1:T(8,128)(2,1)S(1)} %convert_element_type.160) | copy-start | bytes 2359300
  910.0 7.9 copy-start.30
  964.8 22.5 %copy-start.32 = (bf16[768,192]{0,1:T(8,128)(2,1)S(1)}, bf16[768,192]{0,1:T(8,128)(2,1)}, u32[]{:S(2)}) copy-start(bf16[768,192]{0,1:T(8,128)(2,1)} %param.23) | copy-start | bytes 884740
  987.3 20.3 %copy-start.17 = (bf16[2048,192]{0,1:T(8,128)(2,1)}, bf16[2048,192]{0,1:T(8,128)(2,1)S(1)}, u32[]{:S(2)}) copy-start(bf16[2048,192]{0,1:T(8,128)(2,1)S(1)} %convert_element_type.163) | copy-start | bytes 2359300
  1034.1 24.8 %copy-start.33 = (bf16[768,192]{0,1:T(8,128)(2,1)S(1)}, bf16[768,192]{0,1:T(8,128)(2,1)}, u32[]{:S(2)}) copy-start(bf16[768,192]{0,1:T(8,128)(2,1)} %param.24) | copy-start | bytes 884740
  1058.9 8.6 copy-start.19
  1067.5 7.2 copy-start.45
  1067.5 338.7 %all-reduce.16.cloned.1.call-start = ((), (), s32[]{:S(2)}) async-start(), calls=%async_computation.4 | async-start | bytes 14155776 | tf_op jit(solution)/shard_map/psum | solution.py:291
  1074.7 9.7 copy-start.10
  1074.7 9.7 copy-start.16
  1074.7 11.4 copy-start.18
  1406.2 7.9 copy-start.24
  1406.2 9.3 copy-start.23
  1406.2 10.7 copy-start.1
  (39 other events, 107.6 us)
Sparse Core Ops, SparseCore 0:
  104.8 225.5 all-reduce.7
  350.7 221.7 all-reduce.9
  602.1 221.7 all-reduce.11
  1067.7 221.7 all-reduce.13
  1294.5 111.6 all-reduce.15
where the time goes:
time: 1430 us; the launch traced here: 1420 us
  waiting for transfers between devices  948 us (66%)
  local copies, waits for them, and re-layouts  202 us (14%)
  matrix products  169 us (12%)
  other arithmetic  62.7 us (4%)
  blocking collectives  26 us (2%)
  between operations  14.9 us (1%)
    psum x2, waiting for transfers between devices, finish_norm(): summed = lax.psum(partial_sum, 'mp')  447 us
    psum x1, waiting for transfers between devices, on_device(): back_hidden = lax.psum(apply_rows(grad_up_value, up_weight), 'mp')  221 us
    psum x1, waiting for transfers between devices, on_device(): lax.psum(apply_rows(grad_queries, query_weight) + apply_rows(grad_keys, k...  172 us
    psum x1, waiting for transfers between devices, on_device(): summed_all = lax.psum(attn_terms + mlp_terms, 'dp')  109 us
    reshape x2, local copies, waits for them, and re-layouts, attend_back(): grad_listed_k.reshape(split_shape)  43.2 us
    reshape x2, local copies, waits for them, and re-layouts, attend_back(): grad_listed_v.reshape(split_shape)  43 us
    gather x3, local copies, waits for them, and re-layouts, pick_blocks(): source[listed]  29.7 us
    dot_general x6, matrix products, apply_rows(): lax.dot_general(left, weight, (((1,), (1,)), ((), ())), preferred_element...  28.7 us
  transfers between devices with their start and end apart: 5, of which 5 were waited for; matrix products, arithmetic and copies ran while one was open for 2% of the time, Pallas kernels for 0%

commit v1 on v0

--- a/solution.py
+++ b/solution.py
@@ -250,7 +250,7 @@
         grad_mlp_gain,
         grad_mlp_shift,
     )
-    back_hidden = lax.psum(apply_rows(grad_up_value, up_weight), "mp")
+    back_hidden = jnp.sum(lax.all_gather(apply_rows(grad_up_value, up_weight), "mp"), axis=0)
     grad_hidden = grad_mlp_in + back_hidden
     grad_attn_gain = jnp.sum(grad_hidden * normed_attn, 0)
     grad_attn_shift = jnp.sum(grad_hidden, 0)

time: 1430 us -> 1650 us (1.15)
  waiting for transfers between devices: 948 us -> 1150 us
    all_gather x0 -> x1, waiting for transfers between devices: none -> 423 us  [on_device(): lax.all_gather(apply_rows(grad_up_value, up_weight), 'mp')]
    psum x1 -> x0, waiting for transfers between devices: 221 us -> none  [on_device(): back_hidden = lax.psum(apply_rows(grad_up_value, up_weight), 'mp')]
where the time goes in v1:
time: 1650 us; the launch traced here: 1640 us
  waiting for transfers between devices  1150 us (70%)
  local copies, waits for them, and re-layouts  202 us (12%)
  matrix products  169 us (10%)
  other arithmetic  75.2 us (5%)
  blocking collectives  26.4 us (2%)
    psum x2, waiting for transfers between devices, finish_norm(): summed = lax.psum(partial_sum, 'mp')  447 us
    all_gather x1, waiting for transfers between devices, on_device(): lax.all_gather(apply_rows(grad_up_value, up_weight), 'mp')  423 us
    psum x1, waiting for transfers between devices, on_device(): lax.psum(apply_rows(grad_queries, query_weight) + apply_rows(grad_keys, k...  171 us
    psum x1, waiting for transfers between devices, on_device(): summed_all = lax.psum(attn_terms + mlp_terms, 'dp')  109 us
    reshape x2, local copies, waits for them, and re-layouts, attend_back(): grad_listed_v.reshape(split_shape)  43.4 us
    reshape x2, local copies, waits for them, and re-layouts, attend_back(): grad_listed_k.reshape(split_shape)  43 us
  transfers between devices with their start and end apart: 5, of which 5 were waited for; matrix products, arithmetic and copies ran while one was open for 2% of the time, Pallas kernels for 0%

profile of v1, /device:TPU:0, one launch (start us, length us, event | category | flops | bytes accessed | tf_op | source)
XLA Modules:
  0.0 1637.7 jit_solution(13251574246561691506)
XLA Ops:
  38.2 13.9 gather_fusion
  52.1 15.5 gather_fusion.1
  67.6 12.2 multiply_reduce_fusion.1
  79.8 5.9 exponential_reduce_fusion
  85.7 9.5 convolution_convert_fusion.2
  104.5 225.6 %all-reduce.7.cloned.1.call-done = f32[2048,768]{1,0:T(8,128)} async-done(((f32[2048,768]{1,0:T(8,128)}), f32[2048,768]{1,0:T(8,128)}) %all-reduce.7.cloned.1.call-update) | async-done | bytes 6291472 | tf_op jit(solution)/shard_map/psum | solution.py:43
  344.4 5.9 fusion.61
  351.0 221.2 %all-reduce.9.cloned.1.call-done = f32[2048,768]{1,0:T(8,128)} async-done(((f32[2048,768]{1,0:T(8,128)}), f32[2048,768]{1,0:T(8,128)}) %all-reduce.9.cloned.1.call-update) | async-done | bytes 6291472 | tf_op jit(solution)/shard_map/psum | solution.py:45
  572.2 5.7 fusion.63
  583.5 4.9 convert_reduce_fusion.1
  588.4 7.1 convert_reduce_fusion.2
  602.6 423.4 %all-gather.3.cloned.1.call-done = f32[8192,768]{1,0:T(8,128)} async-done(((f32[2048,768]{1,0:T(8,128)}), f32[8192,768]{1,0:T(8,128)}) %all-gather.3.cloned.1.call-update) | async-done | bytes 25165840 | tf_op jit(solution)/shard_map/all_gather | solution.py:253
  1026.0 13.0 reduce_sum.210
  1039.1 8.7 multiply_reduce_fusion.2
  1047.8 5.2 convert_reduce_fusion.3
  1060.7 12.7 multiply_reduce_fusion
  1073.5 10.9 fusion.22
  1093.0 6.9 multiply_convert_fusion
  1102.1 7.2 broadcast_multiply_fusion
  1136.4 16.6 %reshape.244 = f32[2,3,14,8,64,64]{4,3,5,2,1,0:T(8,128)} reshape(f32[2,3,14,512,64]{3,4,2,1,0:T(8,128)} %broadcast_multiply_fusion) | data formatting | bytes 22020096 | tf_op jit(solution)/shard_map/reshape | solution.py:162
  1153.0 26.4 %copy.68 = f32[2,3,14,8,64,64]{5,2,3,4,1,0:T(8,128)} copy(f32[2,3,14,8,64,64]{4,3,5,2,1,0:T(8,128)} %reshape.244) | data formatting | bytes 22020096 | tf_op jit(solution)/shard_map/reshape | solution.py:162
  1179.5 15.6 fusion.21
  1205.7 17.0 %reshape.246 = f32[2,3,14,8,64,64]{4,3,5,2,1,0:T(8,128)} reshape(f32[2,3,14,512,64]{3,4,2,1,0:T(8,128)} %fusion.22) | data formatting | bytes 22020096 | tf_op jit(solution)/shard_map/reshape | solution.py:168
  1222.7 26.4 %copy.73 = f32[2,3,14,8,64,64]{5,2,3,4,1,0:T(8,128)} copy(f32[2,3,14,8,64,64]{4,3,5,2,1,0:T(8,128)} %reshape.246) | data formatting | bytes 22020096 | tf_op jit(solution)/shard_map/reshape | solution.py:168
  1249.2 17.6 %convert_reduce_fusion.4 = (f32[3,64]{1,0:T(4,128)S(1)}, bf16[2,3,16,64,64]{4,2,3,1,0:T(8,128)(2,1)}) fusion(f32[2,3,16,64,64]{4,2,3,1,0:T(8,128)} %copy.75, f32[2,3,14,8,64,64]{5,2,3,4,1,0:T(8,128)} %copy.73, s32[2,3,14,8]{2,3,1,0:T(8,128)S(1)} %pad_add_fusion), kind=kOutput, calls=%fused_computation.51 | convolution fusion | flops 530065728 | bytes 13372800 | tf_op jit(solution)/shard_map/shmcn,shmckd->shnkd/dot_general | solution.py:165
  1273.7 8.6 add_add_fusion
  1282.5 6.9 fusion.74
  1289.4 9.7 fusion.50
  1306.4 26.4 %all-reduce = (f32[192]{0:T(256)}, f32[192]{0:T(256)}, f32[768]{0:T(1024)}, f32[768]{0:T(1024)}, f32[768]{0:T(1024)}, /*index=5*/f32[768]{0:T(1024)}, f32[768]{0:T(1024)}, f32[768]{0:T(1024)}, f32[768]{0:T(1024)}) all-reduce(f32[192]{0:T(256)S(1)} %reduce_sum.216, f32[192]{0:T(256)S(1)} %reduce_sum.218, ...), channel_id=1, replica_groups=mesh['dp'=8,'mp'=4] {'dp'}, use_global_device_ids=true, to_apply=%region_20.0 | all-reduce | flops 5760 | bytes 46080 | tf_op jit(solution)/shard_map/psum | solution.py:291
  1332.8 170.6 %all-reduce.11.cloned.1.call-done = f32[2048,768]{1,0:T(8,128)} async-done(((f32[2048,768]{1,0:T(8,128)}), f32[2048,768]{1,0:T(8,128)}) %all-reduce.11.cloned.1.call-update) | async-done | bytes 6291472 | tf_op jit(solution)/shard_map/psum | solution.py:273
  1503.4 8.1 add.230
  1511.5 108.7 %all-reduce.13.cloned.1.call-done = (f32[768,192]{0,1:T(8,128)}, f32[768,192]{0,1:T(8,128)}, f32[768,192]{0,1:T(8,128)}, f32[192,768]{1,0:T(8,128)}, f32[768,768]{1,0:T(8,128)}, /*index=5*/f32[768,768]{1,0:T(8,128)}) async-done(((f32[768,192]{0,1:T(8,128)}, f32[768,192]{0,1:T(8,128)}, f32[768,192]{0,1:T(8,128)}, f32[192,768]{1,0:T(8,128)}, f32[768,768]{1,0:T(8,128)}, /*index=5*/f32[768,768]{1,0:T(8,128)}), ...) | async-done | bytes 7077904 | tf_op jit(solution)/shard_map/psum | solution.py:291
  (240 shorter events, 148.7 us)
Async XLA Ops:
  7.2 337.3 %copy-start = (bf16[768,768]{1,0:T(8,128)(2,1)S(1)}, bf16[768,768]{1,0:T(8,128)(2,1)}, u32[]{:S(2)}) copy-start(bf16[768,768]{1,0:T(8,128)(2,1)} %param.32) | copy-start | bytes 3538948
  7.2 322.9 %all-reduce.7.cloned.1.call-start = ((), (), s32[]{:S(2)}) async-start(), calls=%async_computation | async-start | bytes 12582912 | tf_op jit(solution)/shard_map/psum | solution.py:43
  17.7 17.1 %copy-start.26 = (bf16[2,3,1,64,64]{4,3,2,1,0:T(8,128)(2,1)}, bf16[2,3,1,64,64]{4,3,2,1,0:T(8,128)(2,1)S(1)}, u32[]{:S(2)}) copy-start(bf16[2,3,1,64,64]{4,3,2,1,0:T(8,128)(2,1)S(1)} %get-tuple-element.52) | copy-start | bytes 147460
  17.7 17.1 %copy-start.28 = (bf16[2,3,1,64,64]{4,3,2,1,0:T(8,128)(2,1)}, bf16[2,3,1,64,64]{4,3,2,1,0:T(8,128)(2,1)S(1)}, u32[]{:S(2)}) copy-start(bf16[2,3,1,64,64]{4,3,2,1,0:T(8,128)(2,1)S(1)} %get-tuple-element.53) | copy-start | bytes 147460
  17.7 9.0 copy-start.31
  52.1 15.5 copy-start.21
  95.2 5.3 copy-start.25
  104.4 467.8 %all-reduce.9.cloned.1.call-start = ((), (), s32[]{:S(2)}) async-start(), calls=%async_computation.1 | async-start | bytes 12582912 | tf_op jit(solution)/shard_map/psum | solution.py:45
  104.5 483.9 %copy-start.44 = (f32[768]{0:T(1024)}, f32[768]{0:T(1024)S(1)}, u32[]{:S(2)}) copy-start(f32[768]{0:T(1024)S(1)} %convert_element_type.146) | copy-start | bytes 9220
  350.3 675.7 %all-gather.3.cloned.1.call-start = ((), (), s32[]{:S(2)}) async-start(), calls=%async_computation.3 | async-start | bytes 31457280 | tf_op jit(solution)/shard_map/all_gather | solution.py:253
  579.8 8.6 slice-start.8
  588.4 7.1 copy-start.11
  601.8 901.6 %all-reduce.11.cloned.1.call-start = ((), (), s32[]{:S(2)}) async-start(), calls=%async_computation.2 | async-start | bytes 12582912 | tf_op jit(solution)/shard_map/psum | solution.py:273
  1073.4 12.0 copy-start.8
  1073.4 12.0 copy-start.35
  1089.3 10.6 slice-start.5
  1093.0 7.0 slice-start.6
  1093.0 7.0 slice-start.7
  1116.7 16.0 copy-start.15
  1124.9 7.9 copy-start.30
  1179.5 22.5 %copy-start.32 = (bf16[768,192]{0,1:T(8,128)(2,1)S(1)}, bf16[768,192]{0,1:T(8,128)(2,1)}, u32[]{:S(2)}) copy-start(bf16[768,192]{0,1:T(8,128)(2,1)} %param.23) | copy-start | bytes 884740
  1202.0 20.7 %copy-start.17 = (bf16[2048,192]{0,1:T(8,128)(2,1)}, bf16[2048,192]{0,1:T(8,128)(2,1)S(1)}, u32[]{:S(2)}) copy-start(bf16[2048,192]{0,1:T(8,128)(2,1)S(1)} %convert_element_type.163) | copy-start | bytes 2359300
  1249.2 24.5 %copy-start.33 = (bf16[768,192]{0,1:T(8,128)(2,1)S(1)}, bf16[768,192]{0,1:T(8,128)(2,1)}, u32[]{:S(2)}) copy-start(bf16[768,192]{0,1:T(8,128)(2,1)} %param.24) | copy-start | bytes 884740
  1273.6 8.6 copy-start.19
  1282.2 7.2 copy-start.45
  1282.3 338.0 %all-reduce.13.cloned.1.call-start = ((), (), s32[]{:S(2)}) async-start(), calls=%async_computation.4 | async-start | bytes 14155776 | tf_op jit(solution)/shard_map/psum | solution.py:291
  1289.4 9.7 copy-start.10
  1289.4 9.7 copy-start.16
  1289.4 11.4 copy-start.18
  1620.2 7.9 copy-start.24
  1620.2 9.3 copy-start.23
  1620.2 10.7 copy-start.1
  (39 other events, 107.7 us)
Sparse Core Ops, SparseCore 0:
  104.5 225.5 all-reduce.6
  350.5 221.7 all-reduce.8
  602.0 424.0 all-gather.2
  1282.4 221.0 all-reduce.10
  1508.5 111.6 all-reduce.12
